TPU v7x, 32 devices: a whole 2x2x4 slice. The times are simulated.
32 devices in a mesh: groups: 2 (over y), section: 4 (over z), tp: 2 (over core), sp: 2 (over x).
Axes of the slice: x: 2, y: 2, z: 4, core: 2. Of those that a mesh axis runs over, the one named last changes fastest.
Arguments:
- hidden: bfloat16 [1024, 6144], P(('groups', 'sp', 'section'), 'tp'), parts along dimension 0, may hold values from -6 to 6
- modulation: float32 [2, 6144], P(None, 'tp'), may hold values from -2 to 2
- time_embed: float32 [12288], P(('groups', 'tp')), parts along dimension 0, may hold values from -2 to 2
- head_weight: bfloat16 [6144, 64], P('tp'), may hold values from -0.078125 to 0.078125
- head_bias: float32 [64], replicated, may hold values from -2 to 2
- noisy: bfloat16 [16, 16, 16, 16], P(('groups', 'sp'), None, 'section'), parts along dimension 0, may hold values from -6 to 6
- step_size: float32 [2], P('groups'), parts along dimension 0, may hold values from 0.2 to 0.6
- latent_mean: float32 [16], replicated, may hold values from -2 to 2
- latent_std: float32 [16], replicated, may hold values from 0.5 to 2
- in_weight: bfloat16 [27, 16, 512], P(None, None, 'tp'), may hold values from -0.3125 to 0.3125
- in_bias: float32 [512], P('tp'), may hold values from -2 to 2
- norm_gain: float32 [512], replicated, may hold values from 0.25 to 1.75
- conv_weight: bfloat16 [27, 512, 512], P(None, 'section', 'tp'), may hold values from -0.0546875 to 0.0546875
- conv_bias: float32 [512], P('tp'), may hold values from -2 to 2
Outputs:
- decoded: bfloat16 [16, 16, 16, 512], P(('groups', 'sp'), None, 'section', 'tp'), parts along dimension 0
There are 2 independent parts, one for each index of `groups`. A program takes and returns all parts, laid end to end along the dimension named above; an argument that names none is the same for every part. Nothing has to cross between parts.
All inputs are finite; a program needn't handle non-finite values.
Results may differ from a plain program's by a relative error of at most 0.006.
Values may be sent and summed in bfloat16 or wider, within the bound.
No kernel may reach another device: no remote copies, remote signals or barrier semaphores. Data moves between devices by JAX's collectives and lax.ppermute only.
A program may use at most 128 MiB of HBM per device.

v0:
```python
import jax
import jax.numpy as jnp
from jax import lax
from jax.sharding import PartitionSpec as P

D = 6144


def padded_2(value, sides, width):
    for axis, dim in sides:
        count, length = (lax.axis_size(axis), value.shape[dim])
        up = [(i, (i + 1) % count) for i in range(count - 1)]
        down = [(j, i) for i, j in up]
        last = lax.slice_in_dim(value, length - width, length, axis=dim)
        leading = lax.slice_in_dim(value, 0, width, axis=dim)
        before = lax.ppermute(last, axis, up)
        after = lax.ppermute(leading, axis, down)
        value = jnp.concatenate([before, value, after], axis=dim)
    return value


def passed_along(value, axis, by):
    count = lax.axis_size(axis)
    pairs = [(i, i + by) for i in range(count) if 0 <= i + by < count]
    return lax.ppermute(value, axis, pairs)


def conv_taps(padded, weight, frames, height, columns):
    channels = padded.shape[3]
    result = jnp.zeros((frames * height * columns, weight.shape[2]), jnp.float32)
    for offset_time in range(3):
        for offset_row in range(3):
            slab = padded[offset_time : offset_time + frames, offset_row : offset_row + height]
            window = jnp.concatenate(
                [slab[:, :, 0:columns], slab[:, :, 1 : columns + 1], slab[:, :, 2 : columns + 2]],
                axis=3,
            )
            first = 9 * offset_time + 3 * offset_row
            taps = weight[first : first + 3].reshape(3 * channels, weight.shape[2])
            result = result + jnp.dot(
                window.reshape(-1, 3 * channels), taps, preferred_element_type=jnp.float32
            )
    return result


def activate(source, gain_vector):
    values = source.astype(jnp.float32)
    squares = jnp.mean(values * values, axis=-1, keepdims=True)
    return jax.nn.silu(values * lax.rsqrt(squares + 1e-06) * gain_vector).astype(jnp.bfloat16)


def pad_rows(source):
    return jnp.pad(source, ((0, 0), (1, 1), (0, 0), (0, 0)))


def shards(
    hidden,
    modulation,
    time_embed,
    head_weight,
    head_bias,
    noisy,
    step_size,
    latent_mean,
    latent_std,
    in_weight,
    in_bias,
    norm_gain,
    conv_weight,
    conv_bias,
):
    frames, height, columns, lat_channels = noisy.shape
    sections = lax.axis_size("section")
    half_channels = in_weight.shape[2]
    values = hidden.astype(jnp.float32)
    row_sums, square_sums = lax.psum(
        (jnp.sum(values, axis=1), jnp.sum(values * values, axis=1)), "tp"
    )
    average = row_sums / D
    variance = square_sums / D - average * average
    shift_term = modulation[0] + time_embed
    scale_term = modulation[1] + time_embed
    modulated = (
        (values - average[:, None]) * lax.rsqrt(variance[:, None] + 1e-06) * (1.0 + scale_term)
        + shift_term
    ).astype(jnp.bfloat16)
    partial_sum = jnp.dot(modulated, head_weight, preferred_element_type=jnp.float32)
    velocity = (lax.psum(partial_sum, "tp") + head_bias).astype(jnp.bfloat16)
    band_rows = velocity.shape[0] * 2 // (columns * sections)
    outgoing = velocity.reshape(band_rows, sections, -1)
    arrived = lax.all_to_all(outgoing, "section", split_axis=1, concat_axis=0, tiled=True)
    latent_field = arrived.reshape(frames, height // 2, columns // 2, 2, 2, lat_channels)
    latent_field = jnp.transpose(latent_field, (0, 1, 3, 2, 4, 5)).reshape(
        frames, height, columns, lat_channels
    )
    latent = (
        (noisy.astype(jnp.float32) - step_size[0] * latent_field.astype(jnp.float32)) * latent_std
        + latent_mean
    ).astype(jnp.bfloat16)
    latent_wide = padded_2(latent, (("section", 2),), 2)
    earlier = passed_along(latent_wide, "sp", 1)
    stacked = pad_rows(jnp.concatenate([earlier, latent_wide], axis=0))
    extended = (conv_taps(stacked, in_weight, frames + 2, height, columns + 2) + in_bias).astype(
        jnp.bfloat16
    )
    extended = extended.reshape(frames + 2, height, columns + 2, half_channels)
    upblock_half = extended[2:, :, 1 : columns + 1]
    extended_full = lax.all_gather(extended, "tp", axis=3, tiled=True)
    normed = activate(extended_full, norm_gain)
    frame_index = lax.axis_index("sp") * frames - 2 + jnp.arange(frames + 2, dtype=jnp.int32)
    column_index = (
        lax.axis_index("section") * columns - 1 + jnp.arange(columns + 2, dtype=jnp.int32)
    )
    inside_cols = (column_index >= 0) & (column_index < columns * sections)
    inside = (frame_index >= 0)[:, None, None, None] & inside_cols[None, None, :, None]
    conv_input = pad_rows(jnp.where(inside, normed, jnp.zeros_like(normed)))
    full_weight = lax.all_gather(conv_weight, "section", axis=1, tiled=True)
    mixed = conv_taps(conv_input, full_weight, frames, height, columns)
    decoded = (
        upblock_half.astype(jnp.float32).reshape(-1, half_channels) + mixed + conv_bias
    ).astype(jnp.bfloat16)
    return decoded.reshape(frames, height, columns, half_channels)


def solution(mesh):
    placed = (
        P(("groups", "sp", "section"), "tp"),
        P(None, "tp"),
        P(("groups", "tp")),
        P("tp", None),
        P(),
        P(("groups", "sp"), None, "section", None),
        P("groups"),
        P(),
        P(),
        P(None, None, "tp"),
        P("tp"),
        P(),
        P(None, "section", "tp"),
        P("tp"),
    )
    return jax.shard_map(
        shards,
        mesh=mesh,
        in_specs=placed,
        out_specs=P(("groups", "sp"), None, "section", "tp"),
        check_vma=False,
    )
```

profile of v0, /device:TPU:0, one launch (start us, length us, event | category | flops | bytes accessed | tf_op | source)
XLA Modules:
  0.0 158.0 jit_solution(14631500808163563009)
XLA Ops:
  7.8 2.6 %all-reduce.2 = (f32[64]{0:T(128)S(1)}, f32[64]{0:T(128)S(1)}) all-reduce(f32[64]{0:T(128)S(1)} %get-tuple-element.6, f32[64]{0:T(128)S(1)} %get-tuple-element.5), channel_id=1, replica_groups=mesh['groups'=2,'section'=4,'tp'=2,'sp'=2] {'tp'}, use_global_device_ids=true, to_apply=%region_3.0 | all-reduce | flops 128 | bytes 1024 | tf_op jit(solution)/shard_map/psum | solution.py:76
  10.8 3.6 %psum.23 = f32[64,64]{1,0:T(8,128)S(1)} all-reduce(f32[64,64]{1,0:T(8,128)S(1)} %fusion.19), channel_id=1, replica_groups=mesh['groups'=2,'section'=4,'tp'=2,'sp'=2] {'tp'}, use_global_device_ids=true, to_apply=%region_4.0 | all-reduce | flops 4096 | bytes 32768 | tf_op jit(solution)/shard_map/psum | solution.py:88
  15.1 6.0 %all-to-all-start = ((bf16[8,4,128]{2,0,1:T(8,128)(2,1)}), bf16[8,4,128]{2,0,1:T(8,128)(2,1)S(1)}, u32[]{:S(2)}, u32[]{:S(2)}) async-start(bf16[8,4,128]{2,0,1:T(8,128)(2,1)} %copy.17), calls=%async_computation | async-start | bytes 16384 | tf_op jit(solution)/shard_map/all_to_all | solution.py:91
  22.5 7.5 %all-to-all-done = bf16[8,4,128]{2,0,1:T(8,128)(2,1)S(1)} async-done(((bf16[8,4,128]{2,0,1:T(8,128)(2,1)}), bf16[8,4,128]{2,0,1:T(8,128)(2,1)S(1)}, u32[]{:S(2)}, u32[]{:S(2)}) %all-to-all-start) | async-done | bytes 8224 | tf_op jit(solution)/shard_map/all_to_all | solution.py:91
  30.4 1.3 collective-permute-start
  31.7 1.3 collective-permute-start.1
  33.9 4.4 %collective-permute-done.1 = bf16[4,16,2,16]{3,2,1,0:T(2,128)(2,1)S(1)} collective-permute-done((bf16[4,16,2,16]{3,2,1,0:T(2,128)(2,1)S(1)}, bf16[4,16,2,16]{3,2,1,0:T(2,128)(2,1)S(1)}, u32[]{:S(2)}, u32[]{:S(2)}) %collective-permute-start.1) | collective-permute-done | bytes 4128 | tf_op jit(solution)/shard_map/ppermute | solution.py:17
  38.5 3.4 %collective-permute-start.2 = (bf16[4,16,8,16]{3,2,1,0:T(8,128)(2,1)S(1)}, bf16[4,16,8,16]{3,2,1,0:T(8,128)(2,1)S(1)}, u32[]{:S(2)}, u32[]{:S(2)}) collective-permute-start(bf16[4,16,8,16]{3,2,1,0:T(8,128)(2,1)S(1)} %pad_maximum_fusion.18), channel_id=1, source_target_pairs={{0,1},{2,3},{4,5},{6,7},{8,9},{10,11},{12,13},{14,15},{16,17},{18,... | collective-permute-start | bytes 49160 | tf_op jit(solution)/shard_map/ppermute | solution.py:25
  42.5 1.9 %collective-permute-done.2 = bf16[4,16,8,16]{3,2,1,0:T(8,128)(2,1)S(1)} collective-permute-done((bf16[4,16,8,16]{3,2,1,0:T(8,128)(2,1)S(1)}, bf16[4,16,8,16]{3,2,1,0:T(8,128)(2,1)S(1)}, u32[]{:S(2)}, u32[]{:S(2)}) %collective-permute-start.2) | collective-permute-done | bytes 16416 | tf_op jit(solution)/shard_map/ppermute | solution.py:25
  47.1 1.3 pad_slice_fusion.1
  50.2 2.2 %pad_maximum_fusion.12 = (bf16[6,16,6,48]{3,2,1,0:T(8,128)(2,1)}, bf16[6,16,6,48]{3,2,1,0:T(8,128)(2,1)S(1)}) fusion(bf16[6,16,6,16]{3,2,1,0:T(8,128)(2,1)S(1)} %get-tuple-element.53, bf16[6,16,6,16]{3,2,1,0:T(8,128)(2,1)S(1)} %get-tuple-element.52, bf16[6,16,6,16]{3,2,1,0:T(8,128)(2,1)S(1)} %get-tuple-element.51, ...), kind=kLoop, calls=%fused_computation.58 | loop fusion | flops 331776 | bytes 221184 | tf_op jit(solution)/shard_map/concatenate | solution.py:34
  52.4 1.7 %reshape.204 = bf16[576,48]{1,0:T(8,128)(2,1)} reshape(bf16[6,16,6,48]{3,2,1,0:T(8,128)(2,1)} %get-tuple-element.91) | data formatting | bytes 110592 | tf_op jit(solution)/shard_map/reshape | solution.py:41
  59.0 2.5 %all_gather.6 = bf16[6,16,6,512]{3,2,1,0:T(8,128)(2,1)S(1)} all-gather(bf16[6,16,6,256]{3,2,1,0:T(8,128)(2,1)S(1)} %reshape.216), channel_id=1, replica_groups=mesh['groups'=2,'section'=4,'tp'=2,'sp'=2] {'tp'}, dimensions={3}, use_global_device_ids=true | all-gather | bytes 884736 | tf_op jit(solution)/shard_map/all_gather | solution.py:108
  62.4 1.4 fusion.26
  64.3 2.3 %pad_slice_fusion.20 = (bf16[4,16,4,512]{3,2,1,0:T(4,128)(2,1)}, bf16[4,16,4,512]{3,2,1,0:T(4,128)(2,1)S(1)}, bf16[4,16,4,512]{3,2,1,0:T(4,128)(2,1)S(1)}, bf16[...) fusion(bf16[6,16,6,512]{3,2,1,0:T(8,128)(2,1)S(1)} %fusion.18), kind=kLoop, calls=%fused_computation.96 | loop fusion | bytes 3670016 | tf_op jit(solution)/shard_map/slice | solution.py:35
  67.2 1.5 pad_maximum_fusion.2
  69.8 1.5 pad_maximum_fusion.3
  72.4 2.5 %pad_slice_fusion.19 = (bf16[4,16,4,512]{3,2,1,0:T(4,128)(2,1)S(1)}, bf16[4,16,4,512]{3,2,1,0:T(4,128)(2,1)}, bf16[4,16,4,512]{3,2,1,0:T(4,128)(2,1)}, bf16[4,16...) fusion(bf16[6,16,6,512]{3,2,1,0:T(8,128)(2,1)S(1)} %fusion.18), kind=kLoop, calls=%fused_computation.95 | loop fusion | bytes 4456448 | tf_op jit(solution)/shard_map/slice | solution.py:35
  75.4 1.5 pad_maximum_fusion.4
  77.9 1.5 pad_maximum_fusion.7
  80.4 1.4 pad_maximum_fusion.5
  82.9 1.4 pad_maximum_fusion.6
  85.5 55.2 %all-gather.2.cloned.1.call-done = bf16[27,512,256]{2,1,0:T(8,128)(2,1)} async-done(((bf16[27,128,256]{2,1,0:T(8,128)(2,1)}), bf16[27,512,256]{2,1,0:T(8,128)(2,1)}) %all-gather.2.cloned.1.call-update) | async-done | bytes 7077904 | tf_op jit(solution)/shard_map/all_gather | solution.py:117
  140.7 3.8 %fusion.25 = (bf16[3,512,256]{2,1,0:T(8,128)(2,1)S(1)}, bf16[3,512,256]{2,1,0:T(8,128)(2,1)S(1)}, bf16[3,512,256]{2,1,0:T(8,128)(2,1)S(1)}, bf16[3,512,256]{2,1,...) fusion(bf16[27,512,256]{2,1,0:T(8,128)(2,1)} %all-gather.2.clon, ...), kind=kLoop, calls=%fused_computation.112 | loop fusion | bytes 14155776 | tf_op jit(solution)/shard_map/slice | solution.py:39
  (150 shorter events, 29.8 us)
Async XLA Ops:
  6.5 3.9 %copy-start = (bf16[3072,64]{0,1:T(8,128)(2,1)S(1)}, bf16[3072,64]{0,1:T(8,128)(2,1)}, u32[]{:S(2)}) copy-start(bf16[3072,64]{0,1:T(8,128)(2,1)} %param.17) | copy-start | bytes 1179652
  6.5 3.9 %copy-start.31 = (f32[3072]{0:T(1024)S(1)}, f32[3072]{0:T(1024)}, u32[]{:S(2)}) copy-start(f32[3072]{0:T(1024)} %param.16) | copy-start | bytes 36868
  6.5 7.9 %copy-start.36 = (f32[64]{0:T(128)S(1)}, f32[64]{0:T(128)}, u32[]{:S(2)}) copy-start(f32[64]{0:T(128)} %param.18) | copy-start | bytes 772
  6.5 14.6 %copy-start.19 = (bf16[27,16,256]{2,1,0:T(8,128)(2,1)S(1)}, bf16[27,16,256]{2,1,0:T(8,128)(2,1)}, u32[]{:S(2)}) copy-start(bf16[27,16,256]{2,1,0:T(8,128)(2,1)} %param.23) | copy-start | bytes 663556
  6.6 134.1 %all-gather.2.cloned.1.call-start = ((), (), s32[]{:S(2)}) async-start(), calls=%async_computation.1 | async-start | bytes 8847360 | tf_op jit(solution)/shard_map/all_gather | solution.py:117
  7.3 22.9 %copy-start.29 = (bf16[4,16,4,16]{3,2,1,0:T(4,128)(2,1)S(1)}, bf16[4,16,4,16]{3,2,1,0:T(4,128)(2,1)}, u32[]{:S(2)}) copy-start(bf16[4,16,4,16]{3,2,1,0:T(4,128)(2,1)} %param.19) | copy-start | bytes 24580
  7.3 22.9 %copy-start.37 = (f32[16]{0:T(128)S(1)}, f32[16]{0:T(128)}, u32[]{:S(2)}) copy-start(f32[16]{0:T(128)} %param.21) | copy-start | bytes 196
  7.3 23.0 %copy-start.38 = (f32[16]{0:T(128)S(1)}, f32[16]{0:T(128)}, u32[]{:S(2)}) copy-start(f32[16]{0:T(128)} %param.22) | copy-start | bytes 196
  15.1 14.9 %all-to-all-start = ((bf16[8,4,128]{2,0,1:T(8,128)(2,1)}), bf16[8,4,128]{2,0,1:T(8,128)(2,1)S(1)}, u32[]{:S(2)}, u32[]{:S(2)}) async-start(bf16[8,4,128]{2,0,1:T(8,128)(2,1)} %copy.17), calls=%async_computation | async-start | bytes 16384 | tf_op jit(solution)/shard_map/all_to_all | solution.py:91
  30.4 3.5 %collective-permute-start = (bf16[4,16,2,16]{3,2,1,0:T(2,128)(2,1)S(1)}, bf16[4,16,2,16]{3,2,1,0:T(2,128)(2,1)S(1)}, u32[]{:S(2)}, u32[]{:S(2)}) collective-permute-start(bf16[4,16,2,16]{3,2,1,0:T(2,128)(2,1)S(1)} %get-tuple-element.81), channel_id=1, source_target_pairs={{0,4},{4,8},{8,12},{1,5},{5,9},{9,13},{2,6},{6,10},{10,14},{3,7},{... | collective-permute-start | bytes 12296 | tf_op jit(solution)/shard_map/ppermute | solution.py:16
  31.7 6.6 %collective-permute-start.1 = (bf16[4,16,2,16]{3,2,1,0:T(2,128)(2,1)S(1)}, bf16[4,16,2,16]{3,2,1,0:T(2,128)(2,1)S(1)}, u32[]{:S(2)}, u32[]{:S(2)}) collective-permute-start(bf16[4,16,2,16]{3,2,1,0:T(2,128)(2,1)S(1)} %get-tuple-element.82), channel_id=1, source_target_pairs={{4,0},{8,4},{12,8},{5,1},{9,5},{13,9},{6,2},{10,6},{14,10},{7,3},{... | collective-permute-start | bytes 12296 | tf_op jit(solution)/shard_map/ppermute | solution.py:17
  38.5 5.9 %collective-permute-start.2 = (bf16[4,16,8,16]{3,2,1,0:T(8,128)(2,1)S(1)}, bf16[4,16,8,16]{3,2,1,0:T(8,128)(2,1)S(1)}, u32[]{:S(2)}, u32[]{:S(2)}) collective-permute-start(bf16[4,16,8,16]{3,2,1,0:T(8,128)(2,1)S(1)} %pad_maximum_fusion.18), channel_id=1, source_target_pairs={{0,1},{2,3},{4,5},{6,7},{8,9},{10,11},{12,13},{14,15},{16,17},{18,... | collective-permute-start | bytes 49160 | tf_op jit(solution)/shard_map/ppermute | solution.py:25
  49.4 4.6 %copy-start.11 = (bf16[6,16,6,16]{3,2,1,0:T(8,128)(2,1)S(1)}, bf16[6,16,6,16]{3,2,1,0:T(8,128)(2,1)}, u32[]{:S(2)}) copy-start(bf16[6,16,6,16]{3,2,1,0:T(8,128)(2,1)} %get-tuple-element.45) | copy-start | bytes 55300
  49.4 4.6 %copy-start.12 = (bf16[6,16,6,16]{3,2,1,0:T(8,128)(2,1)S(1)}, bf16[6,16,6,16]{3,2,1,0:T(8,128)(2,1)}, u32[]{:S(2)}) copy-start(bf16[6,16,6,16]{3,2,1,0:T(8,128)(2,1)} %get-tuple-element.55) | copy-start | bytes 55300
  49.4 4.6 %copy-start.13 = (bf16[6,16,6,16]{3,2,1,0:T(8,128)(2,1)S(1)}, bf16[6,16,6,16]{3,2,1,0:T(8,128)(2,1)}, u32[]{:S(2)}) copy-start(bf16[6,16,6,16]{3,2,1,0:T(8,128)(2,1)} %get-tuple-element.62) | copy-start | bytes 55300
  50.2 4.3 %copy-start.14 = (bf16[6,16,6,48]{3,2,1,0:T(8,128)(2,1)S(1)}, bf16[6,16,6,48]{3,2,1,0:T(8,128)(2,1)}, u32[]{:S(2)}) copy-start(bf16[6,16,6,48]{3,2,1,0:T(8,128)(2,1)} %get-tuple-element.94) | copy-start | bytes 165892
  50.2 4.4 %copy-start.10 = (bf16[6,16,6,16]{3,2,1,0:T(8,128)(2,1)S(1)}, bf16[6,16,6,16]{3,2,1,0:T(8,128)(2,1)}, u32[]{:S(2)}) copy-start(bf16[6,16,6,16]{3,2,1,0:T(8,128)(2,1)} %get-tuple-element.61) | copy-start | bytes 55300
  58.1 3.7 %copy-start.32 = (pred[6,6]{1,0:T(8,128)(4,1)S(1)}, pred[6,6]{1,0:T(8,128)(4,1)}, u32[]{:S(2)}) copy-start(pred[6,6]{1,0:T(8,128)(4,1)} %broadcast_and_fusion) | copy-start | bytes 112
  58.1 3.7 %copy-start.33 = (f32[512]{0:T(512)S(1)}, f32[512]{0:T(512)}, u32[]{:S(2)}) copy-start(f32[512]{0:T(512)} %param.25) | copy-start | bytes 6148
  64.3 2.3 %copy-start.8 = (bf16[4,16,4,512]{3,2,1,0:T(4,128)(2,1)S(1)}, bf16[4,16,4,512]{3,2,1,0:T(4,128)(2,1)}, u32[]{:S(2)}) copy-start(bf16[4,16,4,512]{3,2,1,0:T(4,128)(2,1)} %get-tuple-element.44) | copy-start | bytes 786436
  72.4 2.5 %copy-start.7 = (bf16[4,16,4,512]{3,2,1,0:T(4,128)(2,1)S(1)}, bf16[4,16,4,512]{3,2,1,0:T(4,128)(2,1)}, u32[]{:S(2)}) copy-start(bf16[4,16,4,512]{3,2,1,0:T(4,128)(2,1)} %get-tuple-element.18) | copy-start | bytes 786436
  145.2 1.2 copy-start.2
  146.0 1.2 copy-start.4
  146.8 1.2 copy-start.5
  (20 other events, 18.3 us)
Sparse Core Ops, SparseCore 0:
  8.9 131.6 all-gather.1
where the time goes:
time: 159 us; the launch traced here: 158 us
  waiting for transfers between devices  70.6 us (44%)
  local copies, waits for them, and re-layouts  30.1 us (19%)
  other arithmetic  16.3 us (10%)
  between operations  14.7 us (9%)
  starting transfers between devices  12 us (8%)
  blocking collectives  8.74 us (5%)
  matrix products  5.53 us (3%)
    all_gather x1, waiting for transfers between devices, shards(): full_weight = lax.all_gather(conv_weight, 'section', axis=1, tiled=True)  55.2 us
    concatenate x14, other arithmetic, conv_taps(): jnp.concatenate([slab[:, :, 0:columns], slab[:, :, 1:columns + 1], slab[:...  14.1 us
    reshape x18, local copies, waits for them, and re-layouts, conv_taps(): window.reshape(-1, 3 * channels)  10.7 us
    all_to_all x1, waiting for transfers between devices, shards(): lax.all_to_all(outgoing, 'section', split_axis=1, concat_axis=0, tiled=True)  7.51 us
    all_to_all x1, starting transfers between devices, shards(): lax.all_to_all(outgoing, 'section', split_axis=1, concat_axis=0, tiled=True)  6.02 us
    dot_general x18, matrix products, conv_taps(): jnp.dot(window.reshape(-1, 3 * channels), taps, preferred_element_type=jn...  5.17 us
    slice x4, local copies, waits for them, and re-layouts, conv_taps(): slab[:, :, 0:columns]  4.94 us
    slice x2, local copies, waits for them, and re-layouts, conv_taps(): taps = weight[first:first + 3].reshape(3 * channels, weight.shape[2])  4.44 us
  transfers between devices with their start and end apart: 5, of which 5 were waited for; matrix products, arithmetic and copies ran while one was open for 26% of the time, Pallas kernels for 0%

commit v1 on v0

--- a/solution.py
+++ b/solution.py
@@ -114,7 +114,14 @@
     inside_cols = (column_index >= 0) & (column_index < columns * sections)
     inside = (frame_index >= 0)[:, None, None, None] & inside_cols[None, None, :, None]
     conv_input = pad_rows(jnp.where(inside, normed, jnp.zeros_like(normed)))
-    full_weight = lax.all_gather(conv_weight, "section", axis=1, tiled=True)
+    ring = [conv_weight]
+    for hop in range(3):
+        ring.append(lax.ppermute(ring[-1], "section", [(dev, (dev + 1) % 4) for dev in range(4)]))
+    full_weight = jnp.roll(
+        jnp.concatenate(ring[::-1], axis=1),
+        (lax.axis_index("section") + 1) * ring[0].shape[1],
+        axis=1,
+    )
     mixed = conv_taps(conv_input, full_weight, frames, height, columns)
     decoded = (
         upblock_half.astype(jnp.float32).reshape(-1, half_channels) + mixed + conv_bias

time: 159 us -> 190 us (1.19)
  local copies, waits for them, and re-layouts: 30.1 us -> 51.6 us
  between operations: 14.7 us -> 1.44 us
  waiting for transfers between devices: 70.6 us -> 79.8 us
  other arithmetic: 16.3 us -> 24.9 us
  starting transfers between devices: 12 us -> 15.1 us
  matrix products: 5.53 us -> 7.47 us
    all_gather x1 -> x0, waiting for transfers between devices: 55.2 us -> none  [shards(): full_weight = lax.all_gather(conv_weight, 'section', axis=1, tiled=True)]
    ppermute x0 -> x3, waiting for transfers between devices: none -> 47.8 us  [shards(): lax.ppermute(ring[-1], 'section', [(dev, (dev + 1) % 4) for dev in range(...]
    all_to_all x1, waiting for transfers between devices: 7.51 us -> 25.1 us  [shards(): lax.all_to_all(outgoing, 'section', split_axis=1, concat_axis=0, tiled=True)]
    reshape x18, local copies, waits for them, and re-layouts: 10.7 us -> 24.4 us  [conv_taps(): window.reshape(-1, 3 * channels)]
    unnamed x78 -> x87, local copies, waits for them, and re-layouts: 3.68 us -> 12.4 us
    concatenate x14, other arithmetic: 14.1 us -> 20.7 us  [conv_taps(): jnp.concatenate([slab[:, :, 0:columns], slab[:, :, 1:columns + 1], slab[:...]
    ppermute x0 -> x3, starting transfers between devices: none -> 4.04 us  [shards(): lax.ppermute(ring[-1], 'section', [(dev, (dev + 1) % 4) for dev in range(...]
    slice x2, local copies, waits for them, and re-layouts: 4.44 us -> 1.36 us  [conv_taps(): taps = weight[first:first + 3].reshape(3 * channels, weight.shape[2])]
  transfers between devices with their start and end apart: 5 -> 7, of which waited for: 5 -> 6; matrix products, arithmetic and copies ran while one was open for 26% -> 35% of each run, Pallas kernels for 0% -> 0%
where the time goes in v1:
time: 190 us; the launch traced here: 189 us
  waiting for transfers between devices  79.8 us (42%)
  local copies, waits for them, and re-layouts  51.6 us (27%)
  other arithmetic  24.9 us (13%)
  starting transfers between devices  15.1 us (8%)
  blocking collectives  8.25 us (4%)
  matrix products  7.47 us (4%)
    ppermute x3, waiting for transfers between devices, shards(): lax.ppermute(ring[-1], 'section', [(dev, (dev + 1) % 4) for dev in range(...  47.8 us
    all_to_all x1, waiting for transfers between devices, shards(): lax.all_to_all(outgoing, 'section', split_axis=1, concat_axis=0, tiled=True)  25.1 us
    reshape x18, local copies, waits for them, and re-layouts, conv_taps(): window.reshape(-1, 3 * channels)  24.4 us
    concatenate x14, other arithmetic, conv_taps(): jnp.concatenate([slab[:, :, 0:columns], slab[:, :, 1:columns + 1], slab[:...  20.7 us
    unnamed x87, local copies, waits for them, and re-layouts  12.4 us
    dot_general x18, matrix products, conv_taps(): jnp.dot(window.reshape(-1, 3 * channels), taps, preferred_element_type=jn...  6.13 us
    slice x4, local copies, waits for them, and re-layouts, conv_taps(): slab[:, :, 0:columns]  6.1 us
    ppermute x1, waiting for transfers between devices, padded_2(): after = lax.ppermute(leading, axis, down)  4.23 us
  transfers between devices with their start and end apart: 7, of which 6 were waited for; matrix products, arithmetic and copies ran while one was open for 35% of the time, Pallas kernels for 0%

profile of v1, /device:TPU:0, one launch (start us, length us, event | category | flops | bytes accessed | tf_op | source)
XLA Modules:
  0.0 188.6 jit_solution(10033006741236151485)
XLA Ops:
  0.0 3.1 %collective-permute-start.3 = (bf16[27,128,256]{2,1,0:T(8,128)(2,1)}, bf16[27,128,256]{2,1,0:T(8,128)(2,1)S(1)}, u32[]{:S(2)}, u32[]{:S(2)}) collective-permute-start(bf16[27,128,256]{2,1,0:T(8,128)(2,1)} %param.26), channel_id=1, source_target_pairs={{0,4},{4,8},{8,12},{12,0},{1,5},{5,9},{9,13},{13,1},{2,6},{6,10},{... | collective-permute-start | bytes 5308424 | tf_op jit(solution)/shard_map/ppermute | solution.py:119
  5.2 2.5 %all-reduce.2 = (f32[64]{0:T(128)S(1)}, f32[64]{0:T(128)S(1)}) all-reduce(f32[64]{0:T(128)S(1)} %get-tuple-element.6, f32[64]{0:T(128)S(1)} %get-tuple-element.5), channel_id=1, replica_groups=mesh['groups'=2,'section'=4,'tp'=2,'sp'=2] {'tp'}, use_global_device_ids=true, to_apply=%region_3.0 | all-reduce | flops 128 | bytes 1024 | tf_op jit(solution)/shard_map/psum | solution.py:76
  9.7 3.4 %psum.23 = f32[64,64]{1,0:T(8,128)S(1)} all-reduce(f32[64,64]{1,0:T(8,128)S(1)} %fusion.19), channel_id=1, replica_groups=mesh['groups'=2,'section'=4,'tp'=2,'sp'=2] {'tp'}, use_global_device_ids=true, to_apply=%region_4.0 | all-reduce | flops 4096 | bytes 32768 | tf_op jit(solution)/shard_map/psum | solution.py:88
  13.9 3.9 %all-to-all-start = ((bf16[8,4,128]{2,0,1:T(8,128)(2,1)}), bf16[8,4,128]{2,0,1:T(8,128)(2,1)S(1)}, u32[]{:S(2)}, u32[]{:S(2)}) async-start(bf16[8,4,128]{2,0,1:T(8,128)(2,1)} %copy.17), calls=%async_computation | async-start | bytes 16384 | tf_op jit(solution)/shard_map/all_to_all | solution.py:91
  19.1 25.1 %all-to-all-done = bf16[8,4,128]{2,0,1:T(8,128)(2,1)S(1)} async-done(((bf16[8,4,128]{2,0,1:T(8,128)(2,1)}), bf16[8,4,128]{2,0,1:T(8,128)(2,1)S(1)}, u32[]{:S(2)}, u32[]{:S(2)}) %all-to-all-start) | async-done | bytes 8224 | tf_op jit(solution)/shard_map/all_to_all | solution.py:91
  44.6 2.5 %collective-permute-start = (bf16[4,16,2,16]{3,2,1,0:T(2,128)(2,1)S(1)}, bf16[4,16,2,16]{3,2,1,0:T(2,128)(2,1)S(1)}, u32[]{:S(2)}, u32[]{:S(2)}) collective-permute-start(bf16[4,16,2,16]{3,2,1,0:T(2,128)(2,1)S(1)} %get-tuple-element.81), channel_id=1, source_target_pairs={{0,4},{4,8},{8,12},{1,5},{5,9},{9,13},{2,6},{6,10},{10,14},{3,7},{... | collective-permute-start | bytes 12296 | tf_op jit(solution)/shard_map/ppermute | solution.py:16
  48.6 4.2 %collective-permute-done.1 = bf16[4,16,2,16]{3,2,1,0:T(2,128)(2,1)S(1)} collective-permute-done((bf16[4,16,2,16]{3,2,1,0:T(2,128)(2,1)S(1)}, bf16[4,16,2,16]{3,2,1,0:T(2,128)(2,1)S(1)}, u32[]{:S(2)}, u32[]{:S(2)}) %collective-permute-start.1) | collective-permute-done | bytes 4128 | tf_op jit(solution)/shard_map/ppermute | solution.py:17
  53.0 3.4 %collective-permute-start.2 = (bf16[4,16,8,16]{3,2,1,0:T(8,128)(2,1)S(1)}, bf16[4,16,8,16]{3,2,1,0:T(8,128)(2,1)S(1)}, u32[]{:S(2)}, u32[]{:S(2)}) collective-permute-start(bf16[4,16,8,16]{3,2,1,0:T(8,128)(2,1)S(1)} %pad_maximum_fusion.18), channel_id=1, source_target_pairs={{0,1},{2,3},{4,5},{6,7},{8,9},{10,11},{12,13},{14,15},{16,17},{18,... | collective-permute-start | bytes 49160 | tf_op jit(solution)/shard_map/ppermute | solution.py:25
  56.5 2.4 %collective-permute-done.2 = bf16[4,16,8,16]{3,2,1,0:T(8,128)(2,1)S(1)} collective-permute-done((bf16[4,16,8,16]{3,2,1,0:T(8,128)(2,1)S(1)}, bf16[4,16,8,16]{3,2,1,0:T(8,128)(2,1)S(1)}, u32[]{:S(2)}, u32[]{:S(2)}) %collective-permute-start.2) | collective-permute-done | bytes 16416 | tf_op jit(solution)/shard_map/ppermute | solution.py:25
  65.5 2.4 %pad_maximum_fusion.12 = (bf16[6,16,6,48]{3,2,1,0:T(8,128)(2,1)}, bf16[6,16,6,48]{3,2,1,0:T(8,128)(2,1)}) fusion(bf16[6,16,6,16]{3,2,1,0:T(8,128)(2,1)} %get-tuple-element.53, bf16[6,16,6,16]{3,2,1,0:T(8,128)(2,1)} %get-tuple-element.52, bf16[6,16,6,16]{3,2,1,0:T(8,128)(2,1)} %get-tuple-element.51, bf16[6,16,6,16]{3,2,1,0:T(8,128)(2,1)} %get-tuple-element.54, ...), kind=kLoop, calls=%fused_computation.58 | loop fusion | flops 331776 | bytes 221184 | tf_op jit(solution)/shard_map/concatenate | solution.py:34
  67.9 1.7 reshape.204
  69.6 2.4 %pad_maximum_fusion.10 = (bf16[6,16,6,48]{3,2,1,0:T(8,128)(2,1)S(1)}, bf16[6,16,6,48]{3,2,1,0:T(8,128)(2,1)}) fusion(bf16[6,16,6,16]{3,2,1,0:T(8,128)(2,1)} %get-tuple-element.68, bf16[6,16,6,16]{3,2,1,0:T(8,128)(2,1)} %get-tuple-element.69, bf16[6,16,6,16]{3,2,1,0:T(8,128)(2,1)} %get-tuple-element.70, bf16[6,16,6,16]{3,2,1,0:T(8,128)(2,1)S(1)} %get-tuple-element.65, ...), kind=kLoop, calls=%fused_computation.56 | loop fusion | flops 331776 | bytes 221184 | tf_op jit(solution)/shard_map/concatenate | solution.py:34
  73.9 1.7 reshape.198
  75.6 1.7 reshape.202
  84.6 2.4 %all_gather.3 = bf16[6,16,6,512]{3,2,1,0:T(8,128)(2,1)S(1)} all-gather(bf16[6,16,6,256]{3,2,1,0:T(8,128)(2,1)S(1)} %reshape.216), channel_id=1, replica_groups=mesh['groups'=2,'section'=4,'tp'=2,'sp'=2] {'tp'}, dimensions={3}, use_global_device_ids=true | all-gather | bytes 884736 | tf_op jit(solution)/shard_map/all_gather | solution.py:108
  93.0 2.3 %pad_slice_fusion.20 = (bf16[4,16,4,512]{3,2,1,0:T(4,128)(2,1)}, bf16[4,16,4,512]{3,2,1,0:T(4,128)(2,1)S(1)}, bf16[4,16,4,512]{3,2,1,0:T(4,128)(2,1)S(1)}, bf16[...) fusion(bf16[6,16,6,512]{3,2,1,0:T(8,128)(2,1)S(1)} %fusion.18), kind=kLoop, calls=%fused_computation.113 | loop fusion | bytes 3670016 | tf_op jit(solution)/shard_map/slice | solution.py:35
  96.5 2.3 %reshape.219 = bf16[256,1536]{1,0:T(8,128)(2,1)} reshape(bf16[4,16,4,1536]{3,2,1,0:T(4,128)(2,1)} %pad_maximum_fusion) | data formatting | bytes 1572864 | tf_op jit(solution)/shard_map/reshape | solution.py:41
  98.8 2.3 %pad_maximum_fusion.2 = bf16[4,16,4,1536]{3,2,1,0:T(4,128)(2,1)} fusion(bf16[4,16,4,512]{3,2,1,0:T(4,128)(2,1)} %get-tuple-element.23, bf16[4,16,4,512]{3,2,1,0:T(4,128)(2,1)} %get-tuple-element.22, bf16[4,16,4,512]{3,2,1,0:T(4,128)(2,1)} %get-tuple-element.21), kind=kLoop, calls=%fused_computation.42 | loop fusion | flops 2359296 | bytes 1572864 | tf_op jit(solution)/shard_map/concatenate | solution.py:34
  101.1 2.3 %reshape.223 = bf16[256,1536]{1,0:T(8,128)(2,1)} reshape(bf16[4,16,4,1536]{3,2,1,0:T(4,128)(2,1)} %pad_maximum_fusion.2) | data formatting | bytes 1572864 | tf_op jit(solution)/shard_map/reshape | solution.py:41
  103.4 2.3 %pad_maximum_fusion.3 = bf16[4,16,4,1536]{3,2,1,0:T(4,128)(2,1)} fusion(bf16[4,16,4,512]{3,2,1,0:T(4,128)(2,1)} %get-tuple-element.26, bf16[4,16,4,512]{3,2,1,0:T(4,128)(2,1)} %get-tuple-element.25, bf16[4,16,4,512]{3,2,1,0:T(4,128)(2,1)} %get-tuple-element.24), kind=kLoop, calls=%fused_computation.43 | loop fusion | flops 2359296 | bytes 1572864 | tf_op jit(solution)/shard_map/concatenate | solution.py:34
  105.7 2.3 %reshape.225 = bf16[256,1536]{1,0:T(8,128)(2,1)} reshape(bf16[4,16,4,1536]{3,2,1,0:T(4,128)(2,1)} %pad_maximum_fusion.3) | data formatting | bytes 1572864 | tf_op jit(solution)/shard_map/reshape | solution.py:41
  108.0 22.0 %collective-permute-done.4 = bf16[27,128,256]{2,1,0:T(8,128)(2,1)} collective-permute-done((bf16[27,128,256]{2,1,0:T(8,128)(2,1)S(1)}, bf16[27,128,256]{2,1,0:T(8,128)(2,1)}, u32[]{:S(2)}, u32[]{:S(2)}) %collective-permute-start.4) | collective-permute-done | bytes 1769504 | tf_op jit(solution)/shard_map/ppermute | solution.py:119
  130.1 2.7 %pad_slice_fusion.19 = (bf16[4,16,4,512]{3,2,1,0:T(4,128)(2,1)}, bf16[4,16,4,512]{3,2,1,0:T(4,128)(2,1)}, bf16[4,16,4,512]{3,2,1,0:T(4,128)(2,1)}, bf16[4,16,4,5...) fusion(bf16[6,16,6,512]{3,2,1,0:T(8,128)(2,1)S(1)} %fusion.18), kind=kLoop, calls=%fused_computation.112 | loop fusion | bytes 4456448 | tf_op jit(solution)/shard_map/slice | solution.py:35
  146.2 25.8 %collective-permute-done.5 = bf16[27,128,256]{2,1,0:T(8,128)(2,1)} collective-permute-done((bf16[27,128,256]{2,1,0:T(8,128)(2,1)}, bf16[27,128,256]{2,1,0:T(8,128)(2,1)}, u32[]{:S(2)}, u32[]{:S(2)}) %collective-permute-start.5) | collective-permute-done | bytes 1769504 | tf_op jit(solution)/shard_map/ppermute | solution.py:119
  (163 shorter events, 60.1 us)
Async XLA Ops:
  0.0 8.4 %copy-start = (bf16[3072,64]{0,1:T(8,128)(2,1)S(1)}, bf16[3072,64]{0,1:T(8,128)(2,1)}, u32[]{:S(2)}) copy-start(bf16[3072,64]{0,1:T(8,128)(2,1)} %param.17) | copy-start | bytes 1179652
  0.0 13.2 %copy-start.37 = (f32[64]{0:T(128)S(1)}, f32[64]{0:T(128)}, u32[]{:S(2)}) copy-start(f32[64]{0:T(128)} %param.18) | copy-start | bytes 772
  0.0 17.7 %copy-start.23 = (bf16[27,16,256]{2,1,0:T(8,128)(2,1)S(1)}, bf16[27,16,256]{2,1,0:T(8,128)(2,1)}, u32[]{:S(2)}) copy-start(bf16[27,16,256]{2,1,0:T(8,128)(2,1)} %param.23) | copy-start | bytes 663556
  0.0 44.4 %copy-start.33 = (bf16[4,16,4,16]{3,2,1,0:T(4,128)(2,1)S(1)}, bf16[4,16,4,16]{3,2,1,0:T(4,128)(2,1)}, u32[]{:S(2)}) copy-start(bf16[4,16,4,16]{3,2,1,0:T(4,128)(2,1)} %param.19) | copy-start | bytes 24580
  0.0 44.4 %copy-start.38 = (f32[16]{0:T(128)S(1)}, f32[16]{0:T(128)}, u32[]{:S(2)}) copy-start(f32[16]{0:T(128)} %param.21) | copy-start | bytes 196
  0.0 44.4 %copy-start.39 = (f32[16]{0:T(128)S(1)}, f32[16]{0:T(128)}, u32[]{:S(2)}) copy-start(f32[16]{0:T(128)} %param.22) | copy-start | bytes 196
  0.0 87.2 %collective-permute-start.3 = (bf16[27,128,256]{2,1,0:T(8,128)(2,1)}, bf16[27,128,256]{2,1,0:T(8,128)(2,1)S(1)}, u32[]{:S(2)}, u32[]{:S(2)}) collective-permute-start(bf16[27,128,256]{2,1,0:T(8,128)(2,1)} %param.26), channel_id=1, source_target_pairs={{0,4},{4,8},{8,12},{12,0},{1,5},{5,9},{9,13},{13,1},{2,6},{6,10},{... | collective-permute-start | bytes 5308424 | tf_op jit(solution)/shard_map/ppermute | solution.py:119
  13.9 30.3 %all-to-all-start = ((bf16[8,4,128]{2,0,1:T(8,128)(2,1)}), bf16[8,4,128]{2,0,1:T(8,128)(2,1)S(1)}, u32[]{:S(2)}, u32[]{:S(2)}) async-start(bf16[8,4,128]{2,0,1:T(8,128)(2,1)} %copy.17), calls=%async_computation | async-start | bytes 16384 | tf_op jit(solution)/shard_map/all_to_all | solution.py:91
  44.6 4.1 %collective-permute-start = (bf16[4,16,2,16]{3,2,1,0:T(2,128)(2,1)S(1)}, bf16[4,16,2,16]{3,2,1,0:T(2,128)(2,1)S(1)}, u32[]{:S(2)}, u32[]{:S(2)}) collective-permute-start(bf16[4,16,2,16]{3,2,1,0:T(2,128)(2,1)S(1)} %get-tuple-element.81), channel_id=1, source_target_pairs={{0,4},{4,8},{8,12},{1,5},{5,9},{9,13},{2,6},{6,10},{10,14},{3,7},{... | collective-permute-start | bytes 12296 | tf_op jit(solution)/shard_map/ppermute | solution.py:16
  47.1 5.8 %collective-permute-start.1 = (bf16[4,16,2,16]{3,2,1,0:T(2,128)(2,1)S(1)}, bf16[4,16,2,16]{3,2,1,0:T(2,128)(2,1)S(1)}, u32[]{:S(2)}, u32[]{:S(2)}) collective-permute-start(bf16[4,16,2,16]{3,2,1,0:T(2,128)(2,1)S(1)} %get-tuple-element.82), channel_id=1, source_target_pairs={{4,0},{8,4},{12,8},{5,1},{9,5},{13,9},{6,2},{10,6},{14,10},{7,3},{... | collective-permute-start | bytes 12296 | tf_op jit(solution)/shard_map/ppermute | solution.py:17
  53.0 5.9 %collective-permute-start.2 = (bf16[4,16,8,16]{3,2,1,0:T(8,128)(2,1)S(1)}, bf16[4,16,8,16]{3,2,1,0:T(8,128)(2,1)S(1)}, u32[]{:S(2)}, u32[]{:S(2)}) collective-permute-start(bf16[4,16,8,16]{3,2,1,0:T(8,128)(2,1)S(1)} %pad_maximum_fusion.18), channel_id=1, source_target_pairs={{0,1},{2,3},{4,5},{6,7},{8,9},{10,11},{12,13},{14,15},{16,17},{18,... | collective-permute-start | bytes 49160 | tf_op jit(solution)/shard_map/ppermute | solution.py:25
  72.7 7.6 %copy-start.16 = (bf16[6,16,6,16]{3,2,1,0:T(8,128)(2,1)S(1)}, bf16[6,16,6,16]{3,2,1,0:T(8,128)(2,1)}, u32[]{:S(2)}) copy-start(bf16[6,16,6,16]{3,2,1,0:T(8,128)(2,1)} %get-tuple-element.55) | copy-start | bytes 55300
  72.7 7.6 %copy-start.17 = (bf16[6,16,6,16]{3,2,1,0:T(8,128)(2,1)S(1)}, bf16[6,16,6,16]{3,2,1,0:T(8,128)(2,1)}, u32[]{:S(2)}) copy-start(bf16[6,16,6,16]{3,2,1,0:T(8,128)(2,1)} %get-tuple-element.62) | copy-start | bytes 55300
  72.7 7.6 %copy-start.18 = (bf16[6,16,6,16]{3,2,1,0:T(8,128)(2,1)S(1)}, bf16[6,16,6,16]{3,2,1,0:T(8,128)(2,1)}, u32[]{:S(2)}) copy-start(bf16[6,16,6,16]{3,2,1,0:T(8,128)(2,1)} %get-tuple-element.45) | copy-start | bytes 55300
  73.9 6.8 %copy-start.24 = (bf16[3,16,256]{2,1,0:T(8,128)(2,1)S(1)}, bf16[3,16,256]{2,1,0:T(8,128)(2,1)}, u32[]{:S(2)}) copy-start(bf16[3,16,256]{2,1,0:T(8,128)(2,1)} %get-tuple-element.79) | copy-start | bytes 73732
  75.6 6.3 %copy-start.21 = (bf16[576,48]{1,0:T(8,128)(2,1)S(1)}, bf16[576,48]{1,0:T(8,128)(2,1)}, u32[]{:S(2)}) copy-start(bf16[576,48]{1,0:T(8,128)(2,1)} %reshape.200) | copy-start | bytes 165892
  75.6 6.3 %copy-start.32 = (bf16[3,16,256]{2,1,0:T(8,128)(2,1)S(1)}, bf16[3,16,256]{2,1,0:T(8,128)(2,1)}, u32[]{:S(2)}) copy-start(bf16[3,16,256]{2,1,0:T(8,128)(2,1)} %get-tuple-element.78) | copy-start | bytes 73732
  84.5 3.7 %copy-start.34 = (f32[512]{0:T(512)S(1)}, f32[512]{0:T(512)}, u32[]{:S(2)}) copy-start(f32[512]{0:T(512)} %param.25) | copy-start | bytes 6148
  84.6 2.7 %copy-start.11 = (bf16[6,16,6,256]{3,2,1,0:T(8,128)(2,1)}, bf16[6,16,6,256]{3,2,1,0:T(8,128)(2,1)S(1)}, u32[]{:S(2)}) copy-start(bf16[6,16,6,256]{3,2,1,0:T(8,128)(2,1)S(1)} %reshape.216) | copy-start | bytes 884740
  87.3 42.8 %collective-permute-start.4 = (bf16[27,128,256]{2,1,0:T(8,128)(2,1)S(1)}, bf16[27,128,256]{2,1,0:T(8,128)(2,1)}, u32[]{:S(2)}, u32[]{:S(2)}) collective-permute-start(bf16[27,128,256]{2,1,0:T(8,128)(2,1)S(1)} %collective-permute-done.3), channel_id=1, source_target_pairs={{0,4},{4,8},{8,12},{12,0},{1,5},{5,9},{9,13},{13,1},{2,6},{6,10},{... | collective-permute-start | bytes 5308424 | tf_op jit(solution)/shard_map/ppermute | solution.py:119
  92.9 2.3 %copy-start.14 = (bf16[4,16,4,512]{3,2,1,0:T(4,128)(2,1)S(1)}, bf16[4,16,4,512]{3,2,1,0:T(4,128)(2,1)}, u32[]{:S(2)}) copy-start(bf16[4,16,4,512]{3,2,1,0:T(4,128)(2,1)} %get-tuple-element.44) | copy-start | bytes 786436
  108.0 24.8 %copy-start.12 = (bf16[4,16,4,512]{3,2,1,0:T(4,128)(2,1)S(1)}, bf16[4,16,4,512]{3,2,1,0:T(4,128)(2,1)}, u32[]{:S(2)}) copy-start(bf16[4,16,4,512]{3,2,1,0:T(4,128)(2,1)} %get-tuple-element.39) | copy-start | bytes 786436
  108.0 24.8 %copy-start.13 = (bf16[4,16,4,512]{3,2,1,0:T(4,128)(2,1)S(1)}, bf16[4,16,4,512]{3,2,1,0:T(4,128)(2,1)}, u32[]{:S(2)}) copy-start(bf16[4,16,4,512]{3,2,1,0:T(4,128)(2,1)} %get-tuple-element.40) | copy-start | bytes 786436
  130.1 41.9 %collective-permute-start.5 = (bf16[27,128,256]{2,1,0:T(8,128)(2,1)}, bf16[27,128,256]{2,1,0:T(8,128)(2,1)}, u32[]{:S(2)}, u32[]{:S(2)}) collective-permute-start(bf16[27,128,256]{2,1,0:T(8,128)(2,1)} %collective-permute-done.4), channel_id=1, source_target_pairs={{0,4},{4,8},{8,12},{12,0},{1,5},{5,9},{9,13},{13,1},{2,6},{6,10},{... | collective-permute-start | bytes 5308424 | tf_op jit(solution)/shard_map/ppermute | solution.py:119
  (23 other events, 27.7 us)
